TPU v7x, 256 devices: a whole 4x4x8 slice. The times are simulated.
256 devices in a mesh: ka: 8 (over y_hi, x), band: 32 (over y_lo, z, core).
Axes of the slice: x: 4, y: 4 (y_hi: 2, y_lo: 2; y = y_hi * 2 + y_lo), z: 8, core: 2. Of those that a mesh axis runs over, the one named last changes fastest.
Arguments:
- targets: float32 [256, 2, 24, 576], P(('ka', 'band')), may hold values from -6 to 6
- occupied: bfloat16 [256, 2, 24, 576], P(('ka', 'band')), may hold values from -3 to 3
- kernels: float32 [16, 24, 576], replicated, may hold values from 0.1 to 2
- partner: int32 [8], replicated, may hold values from 0 to 7, as said below
- kernel_index: int32 [16, 16], replicated, may hold values from 0 to 15
Outputs:
- exchange: float32 [256, 2, 24, 576], P(('ka', 'band'))
Inputs may be any that keep to these rules, and one draw needn't show every extreme that they name: partner is a permutation of the groups.
All inputs are finite; a program needn't handle non-finite values.
Results may differ from a plain program's by a relative error of at most 0.0003.
Values may be sent and summed in bfloat16 or wider, within the bound.
A program may use at most 64 MiB of HBM per device.

v0:
```python
import jax
import jax.numpy as jnp
from jax import lax
from jax.sharding import PartitionSpec as P

GRID = 24
KPT_DEV = 2


def passed_along(array, axis, by):
    peers = lax.axis_size(axis)
    return lax.ppermute(array, axis, [(i, (i + by) % peers) for i in range(peers)])


def spectral_tables(grid_size):
    positions = jnp.arange(grid_size, dtype=jnp.int32)
    products = positions[:, None] * positions[None, :] % grid_size
    angles = products.astype(jnp.float32) * (2.0 * jnp.pi / grid_size)
    factor = 1.0 / jnp.sqrt(jnp.float32(grid_size))
    return (jnp.cos(angles) * factor, jnp.sin(angles) * factor)


def rotate_apply(source_field, matrix):
    batch_count, grid_size, plane_size = source_field.shape
    result = lax.dot_general(
        source_field,
        matrix,
        (((1,), (1,)), ((), ())),
        precision=lax.Precision.HIGHEST,
        preferred_element_type=jnp.float32,
    )
    return result.reshape(batch_count, grid_size, plane_size)


def transform(real_part, imag_part, cosine_table, sine_table, direction):
    for repeat in range(3):
        real_part, imag_part = (
            rotate_apply(real_part, cosine_table) - direction * rotate_apply(imag_part, sine_table),
            rotate_apply(imag_part, cosine_table) + direction * rotate_apply(real_part, sine_table),
        )
    return (real_part, imag_part)


def pair_term(orbital, target_real, target_imag, kernel, cosine_table, sine_table):
    orbital_values = orbital.astype(jnp.float32)
    orbital_real = orbital_values[0, 0]
    orbital_imag = orbital_values[0, 1]
    dens_real = orbital_real * target_real + orbital_imag * target_imag
    dens_imag = orbital_real * target_imag - orbital_imag * target_real
    spec_real, spec_imag = transform(dens_real, dens_imag, cosine_table, sine_table, -1.0)
    pot_real, pot_imag = transform(
        kernel * spec_real, kernel * spec_imag, cosine_table, sine_table, 1.0
    )
    return (
        orbital_real * pot_real - orbital_imag * pot_imag,
        orbital_real * pot_imag + orbital_imag * pot_real,
    )


def shards(targets, occupied, kernels, partner, kernel_index):
    band_count = lax.axis_size("band")
    per_kpoint = band_count // KPT_DEV
    my_group = lax.axis_index("ka")
    position = lax.axis_index("band")
    kpoint = my_group * KPT_DEV + position // per_kpoint
    cosine_table, sine_table = spectral_tables(GRID)
    target_real = targets[:, 0]
    target_imag = targets[:, 1]
    everyone = lax.all_gather(occupied, "ka", axis=0, tiled=True)
    partner_group = partner[my_group]
    visitor = lax.dynamic_slice_in_dim(everyone, partner_group, 1, 0)

    def contribute(totals, orbital, source_band):
        source_k = partner_group * KPT_DEV + source_band // per_kpoint
        table_row = kernel_index[kpoint, source_k]
        kernel = lax.dynamic_index_in_dim(kernels, table_row, 0, keepdims=False)
        more_real, more_imag = pair_term(
            orbital, target_real, target_imag, kernel, cosine_table, sine_table
        )
        return (totals[0] - more_real, totals[1] - more_imag)

    empty_field = jnp.zeros_like(target_real)
    totals = contribute((empty_field, empty_field), visitor, position)

    def onward(number, carried):
        current, summed = carried
        current = passed_along(current, "band", 1)
        return (current, contribute(summed, current, (position - number) % band_count))

    current, totals = lax.fori_loop(1, band_count, onward, (visitor, totals))
    return jnp.stack(totals, axis=1)


def solution(mesh):
    return jax.shard_map(
        shards,
        mesh=mesh,
        in_specs=(
            P(("ka", "band"), None, None, None),
            P(("ka", "band"), None, None, None),
            P(),
            P(),
            P(),
        ),
        out_specs=P(("ka", "band"), None, None, None),
        check_vma=False,
    )
```

profile of v0, /device:TPU:2, one launch (start us, length us, event | category | flops | bytes accessed | tf_op | source)
XLA Modules:
  0.0 548.9 jit_solution(14453901876114819552)
XLA Ops:
  6.8 35.1 %all_gather.3 = bf16[8,2,24,576]{3,2,1,0:T(8,128)(2,1)S(1)} all-gather(bf16[1,2,24,576]{3,2,1,0:T(8,128)(2,1)S(1)} %copy-done.2), channel_id=1, replica_groups=mesh['ka'=8,'band'=32] {'ka'}, dimensions={0}, use_global_device_ids=true | all-gather | bytes 497664 | tf_op jit(solution)/shard_map/all_gather | solution.py:69
  52.9 495.4 %while.21 = (s32[]{:T(128)}, bf16[1,2,24,576]{3,2,1,0:T(8,128)(2,1)S(1)}, f32[1,24,576]{2,1,0:T(8,128)S(1)}, f32[1,24,576]{2,1,0:T(8,128)S(1)}, s32[]{:T(128)}, ...) while((s32[]{:T(128)}, ...), condition=%wide.region_1.2_spmd.clone.clone, body=%wide.region_0.1_spmd.clone.clone.sunk | while | flops 96215040 | bytes 7526992 | solution.py:90
  56.4 2.5 collective-permute-done
  72.4 2.5 collective-permute-done
  88.4 2.5 collective-permute-done
  104.3 2.5 collective-permute-done
  120.3 2.5 collective-permute-done
  136.3 2.5 collective-permute-done
  152.3 2.5 collective-permute-done
  168.2 2.5 collective-permute-done
  184.2 2.5 collective-permute-done
  200.2 2.5 collective-permute-done
  216.2 2.5 collective-permute-done
  232.1 2.5 collective-permute-done
  248.1 2.5 collective-permute-done
  264.1 2.5 collective-permute-done
  280.1 2.5 collective-permute-done
  296.0 2.5 collective-permute-done
  312.0 2.5 collective-permute-done
  328.0 2.5 collective-permute-done
  344.0 2.5 collective-permute-done
  359.9 2.5 collective-permute-done
  375.9 2.5 collective-permute-done
  391.9 2.5 collective-permute-done
  407.9 2.5 collective-permute-done
  423.8 2.5 collective-permute-done
  439.8 2.5 collective-permute-done
  471.8 2.5 collective-permute-done
  487.7 2.5 collective-permute-done
  503.7 2.5 collective-permute-done
  519.7 2.5 collective-permute-done
  535.7 2.5 collective-permute-done
  (1735 shorter events, 362.3 us)
Async XLA Ops:
  0.0 6.8 %copy-start.2 = (bf16[1,2,24,576]{3,2,1,0:T(8,128)(2,1)S(1)}, bf16[1,2,24,576]{3,2,1,0:T(8,128)(2,1)}, u32[]{:S(2)}) copy-start(bf16[1,2,24,576]{3,2,1,0:T(8,128)(2,1)} %param.8) | copy-start | bytes 165892
  53.1 5.8 %collective-permute-start = (bf16[1,2,24,576]{3,2,1,0:T(8,128)(2,1)S(1)}, bf16[1,2,24,576]{3,2,1,0:T(8,128)(2,1)S(1)}, u32[]{:S(2)}, u32[]{:S(2)}) collective-permute-start(bf16[1,2,24,576]{3,2,1,0:T(8,128)(2,1)S(1)} %get-tuple-element.598), channel_id=1, source_target_pairs={{0,1},{1,2},{2,3},{3,4},{4,5},{5,6},{6,7},{7,8},{8,9},{9,10},{10,1... | collective-permute-start | bytes 165896 | tf_op jit(solution)/shard_map/while/body/eval_jaxpr/ppermute | solution.py:12
  69.0 5.8 %collective-permute-start = (bf16[1,2,24,576]{3,2,1,0:T(8,128)(2,1)S(1)}, bf16[1,2,24,576]{3,2,1,0:T(8,128)(2,1)S(1)}, u32[]{:S(2)}, u32[]{:S(2)}) collective-permute-start(bf16[1,2,24,576]{3,2,1,0:T(8,128)(2,1)S(1)} %get-tuple-element.598), channel_id=1, source_target_pairs={{0,1},{1,2},{2,3},{3,4},{4,5},{5,6},{6,7},{7,8},{8,9},{9,10},{10,1... | collective-permute-start | bytes 165896 | tf_op jit(solution)/shard_map/while/body/eval_jaxpr/ppermute | solution.py:12
  85.0 5.8 %collective-permute-start = (bf16[1,2,24,576]{3,2,1,0:T(8,128)(2,1)S(1)}, bf16[1,2,24,576]{3,2,1,0:T(8,128)(2,1)S(1)}, u32[]{:S(2)}, u32[]{:S(2)}) collective-permute-start(bf16[1,2,24,576]{3,2,1,0:T(8,128)(2,1)S(1)} %get-tuple-element.598), channel_id=1, source_target_pairs={{0,1},{1,2},{2,3},{3,4},{4,5},{5,6},{6,7},{7,8},{8,9},{9,10},{10,1... | collective-permute-start | bytes 165896 | tf_op jit(solution)/shard_map/while/body/eval_jaxpr/ppermute | solution.py:12
  101.0 5.8 %collective-permute-start = (bf16[1,2,24,576]{3,2,1,0:T(8,128)(2,1)S(1)}, bf16[1,2,24,576]{3,2,1,0:T(8,128)(2,1)S(1)}, u32[]{:S(2)}, u32[]{:S(2)}) collective-permute-start(bf16[1,2,24,576]{3,2,1,0:T(8,128)(2,1)S(1)} %get-tuple-element.598), channel_id=1, source_target_pairs={{0,1},{1,2},{2,3},{3,4},{4,5},{5,6},{6,7},{7,8},{8,9},{9,10},{10,1... | collective-permute-start | bytes 165896 | tf_op jit(solution)/shard_map/while/body/eval_jaxpr/ppermute | solution.py:12
  117.0 5.8 %collective-permute-start = (bf16[1,2,24,576]{3,2,1,0:T(8,128)(2,1)S(1)}, bf16[1,2,24,576]{3,2,1,0:T(8,128)(2,1)S(1)}, u32[]{:S(2)}, u32[]{:S(2)}) collective-permute-start(bf16[1,2,24,576]{3,2,1,0:T(8,128)(2,1)S(1)} %get-tuple-element.598), channel_id=1, source_target_pairs={{0,1},{1,2},{2,3},{3,4},{4,5},{5,6},{6,7},{7,8},{8,9},{9,10},{10,1... | collective-permute-start | bytes 165896 | tf_op jit(solution)/shard_map/while/body/eval_jaxpr/ppermute | solution.py:12
  132.9 5.8 %collective-permute-start = (bf16[1,2,24,576]{3,2,1,0:T(8,128)(2,1)S(1)}, bf16[1,2,24,576]{3,2,1,0:T(8,128)(2,1)S(1)}, u32[]{:S(2)}, u32[]{:S(2)}) collective-permute-start(bf16[1,2,24,576]{3,2,1,0:T(8,128)(2,1)S(1)} %get-tuple-element.598), channel_id=1, source_target_pairs={{0,1},{1,2},{2,3},{3,4},{4,5},{5,6},{6,7},{7,8},{8,9},{9,10},{10,1... | collective-permute-start | bytes 165896 | tf_op jit(solution)/shard_map/while/body/eval_jaxpr/ppermute | solution.py:12
  148.9 5.8 %collective-permute-start = (bf16[1,2,24,576]{3,2,1,0:T(8,128)(2,1)S(1)}, bf16[1,2,24,576]{3,2,1,0:T(8,128)(2,1)S(1)}, u32[]{:S(2)}, u32[]{:S(2)}) collective-permute-start(bf16[1,2,24,576]{3,2,1,0:T(8,128)(2,1)S(1)} %get-tuple-element.598), channel_id=1, source_target_pairs={{0,1},{1,2},{2,3},{3,4},{4,5},{5,6},{6,7},{7,8},{8,9},{9,10},{10,1... | collective-permute-start | bytes 165896 | tf_op jit(solution)/shard_map/while/body/eval_jaxpr/ppermute | solution.py:12
  164.9 5.8 %collective-permute-start = (bf16[1,2,24,576]{3,2,1,0:T(8,128)(2,1)S(1)}, bf16[1,2,24,576]{3,2,1,0:T(8,128)(2,1)S(1)}, u32[]{:S(2)}, u32[]{:S(2)}) collective-permute-start(bf16[1,2,24,576]{3,2,1,0:T(8,128)(2,1)S(1)} %get-tuple-element.598), channel_id=1, source_target_pairs={{0,1},{1,2},{2,3},{3,4},{4,5},{5,6},{6,7},{7,8},{8,9},{9,10},{10,1... | collective-permute-start | bytes 165896 | tf_op jit(solution)/shard_map/while/body/eval_jaxpr/ppermute | solution.py:12
  180.9 5.8 %collective-permute-start = (bf16[1,2,24,576]{3,2,1,0:T(8,128)(2,1)S(1)}, bf16[1,2,24,576]{3,2,1,0:T(8,128)(2,1)S(1)}, u32[]{:S(2)}, u32[]{:S(2)}) collective-permute-start(bf16[1,2,24,576]{3,2,1,0:T(8,128)(2,1)S(1)} %get-tuple-element.598), channel_id=1, source_target_pairs={{0,1},{1,2},{2,3},{3,4},{4,5},{5,6},{6,7},{7,8},{8,9},{9,10},{10,1... | collective-permute-start | bytes 165896 | tf_op jit(solution)/shard_map/while/body/eval_jaxpr/ppermute | solution.py:12
  196.8 5.8 %collective-permute-start = (bf16[1,2,24,576]{3,2,1,0:T(8,128)(2,1)S(1)}, bf16[1,2,24,576]{3,2,1,0:T(8,128)(2,1)S(1)}, u32[]{:S(2)}, u32[]{:S(2)}) collective-permute-start(bf16[1,2,24,576]{3,2,1,0:T(8,128)(2,1)S(1)} %get-tuple-element.598), channel_id=1, source_target_pairs={{0,1},{1,2},{2,3},{3,4},{4,5},{5,6},{6,7},{7,8},{8,9},{9,10},{10,1... | collective-permute-start | bytes 165896 | tf_op jit(solution)/shard_map/while/body/eval_jaxpr/ppermute | solution.py:12
  212.8 5.8 %collective-permute-start = (bf16[1,2,24,576]{3,2,1,0:T(8,128)(2,1)S(1)}, bf16[1,2,24,576]{3,2,1,0:T(8,128)(2,1)S(1)}, u32[]{:S(2)}, u32[]{:S(2)}) collective-permute-start(bf16[1,2,24,576]{3,2,1,0:T(8,128)(2,1)S(1)} %get-tuple-element.598), channel_id=1, source_target_pairs={{0,1},{1,2},{2,3},{3,4},{4,5},{5,6},{6,7},{7,8},{8,9},{9,10},{10,1... | collective-permute-start | bytes 165896 | tf_op jit(solution)/shard_map/while/body/eval_jaxpr/ppermute | solution.py:12
  228.8 5.8 %collective-permute-start = (bf16[1,2,24,576]{3,2,1,0:T(8,128)(2,1)S(1)}, bf16[1,2,24,576]{3,2,1,0:T(8,128)(2,1)S(1)}, u32[]{:S(2)}, u32[]{:S(2)}) collective-permute-start(bf16[1,2,24,576]{3,2,1,0:T(8,128)(2,1)S(1)} %get-tuple-element.598), channel_id=1, source_target_pairs={{0,1},{1,2},{2,3},{3,4},{4,5},{5,6},{6,7},{7,8},{8,9},{9,10},{10,1... | collective-permute-start | bytes 165896 | tf_op jit(solution)/shard_map/while/body/eval_jaxpr/ppermute | solution.py:12
  244.8 5.8 %collective-permute-start = (bf16[1,2,24,576]{3,2,1,0:T(8,128)(2,1)S(1)}, bf16[1,2,24,576]{3,2,1,0:T(8,128)(2,1)S(1)}, u32[]{:S(2)}, u32[]{:S(2)}) collective-permute-start(bf16[1,2,24,576]{3,2,1,0:T(8,128)(2,1)S(1)} %get-tuple-element.598), channel_id=1, source_target_pairs={{0,1},{1,2},{2,3},{3,4},{4,5},{5,6},{6,7},{7,8},{8,9},{9,10},{10,1... | collective-permute-start | bytes 165896 | tf_op jit(solution)/shard_map/while/body/eval_jaxpr/ppermute | solution.py:12
  260.7 5.8 %collective-permute-start = (bf16[1,2,24,576]{3,2,1,0:T(8,128)(2,1)S(1)}, bf16[1,2,24,576]{3,2,1,0:T(8,128)(2,1)S(1)}, u32[]{:S(2)}, u32[]{:S(2)}) collective-permute-start(bf16[1,2,24,576]{3,2,1,0:T(8,128)(2,1)S(1)} %get-tuple-element.598), channel_id=1, source_target_pairs={{0,1},{1,2},{2,3},{3,4},{4,5},{5,6},{6,7},{7,8},{8,9},{9,10},{10,1... | collective-permute-start | bytes 165896 | tf_op jit(solution)/shard_map/while/body/eval_jaxpr/ppermute | solution.py:12
  276.7 5.8 %collective-permute-start = (bf16[1,2,24,576]{3,2,1,0:T(8,128)(2,1)S(1)}, bf16[1,2,24,576]{3,2,1,0:T(8,128)(2,1)S(1)}, u32[]{:S(2)}, u32[]{:S(2)}) collective-permute-start(bf16[1,2,24,576]{3,2,1,0:T(8,128)(2,1)S(1)} %get-tuple-element.598), channel_id=1, source_target_pairs={{0,1},{1,2},{2,3},{3,4},{4,5},{5,6},{6,7},{7,8},{8,9},{9,10},{10,1... | collective-permute-start | bytes 165896 | tf_op jit(solution)/shard_map/while/body/eval_jaxpr/ppermute | solution.py:12
  292.7 5.8 %collective-permute-start = (bf16[1,2,24,576]{3,2,1,0:T(8,128)(2,1)S(1)}, bf16[1,2,24,576]{3,2,1,0:T(8,128)(2,1)S(1)}, u32[]{:S(2)}, u32[]{:S(2)}) collective-permute-start(bf16[1,2,24,576]{3,2,1,0:T(8,128)(2,1)S(1)} %get-tuple-element.598), channel_id=1, source_target_pairs={{0,1},{1,2},{2,3},{3,4},{4,5},{5,6},{6,7},{7,8},{8,9},{9,10},{10,1... | collective-permute-start | bytes 165896 | tf_op jit(solution)/shard_map/while/body/eval_jaxpr/ppermute | solution.py:12
  308.7 5.8 %collective-permute-start = (bf16[1,2,24,576]{3,2,1,0:T(8,128)(2,1)S(1)}, bf16[1,2,24,576]{3,2,1,0:T(8,128)(2,1)S(1)}, u32[]{:S(2)}, u32[]{:S(2)}) collective-permute-start(bf16[1,2,24,576]{3,2,1,0:T(8,128)(2,1)S(1)} %get-tuple-element.598), channel_id=1, source_target_pairs={{0,1},{1,2},{2,3},{3,4},{4,5},{5,6},{6,7},{7,8},{8,9},{9,10},{10,1... | collective-permute-start | bytes 165896 | tf_op jit(solution)/shard_map/while/body/eval_jaxpr/ppermute | solution.py:12
  324.6 5.8 %collective-permute-start = (bf16[1,2,24,576]{3,2,1,0:T(8,128)(2,1)S(1)}, bf16[1,2,24,576]{3,2,1,0:T(8,128)(2,1)S(1)}, u32[]{:S(2)}, u32[]{:S(2)}) collective-permute-start(bf16[1,2,24,576]{3,2,1,0:T(8,128)(2,1)S(1)} %get-tuple-element.598), channel_id=1, source_target_pairs={{0,1},{1,2},{2,3},{3,4},{4,5},{5,6},{6,7},{7,8},{8,9},{9,10},{10,1... | collective-permute-start | bytes 165896 | tf_op jit(solution)/shard_map/while/body/eval_jaxpr/ppermute | solution.py:12
  340.6 5.8 %collective-permute-start = (bf16[1,2,24,576]{3,2,1,0:T(8,128)(2,1)S(1)}, bf16[1,2,24,576]{3,2,1,0:T(8,128)(2,1)S(1)}, u32[]{:S(2)}, u32[]{:S(2)}) collective-permute-start(bf16[1,2,24,576]{3,2,1,0:T(8,128)(2,1)S(1)} %get-tuple-element.598), channel_id=1, source_target_pairs={{0,1},{1,2},{2,3},{3,4},{4,5},{5,6},{6,7},{7,8},{8,9},{9,10},{10,1... | collective-permute-start | bytes 165896 | tf_op jit(solution)/shard_map/while/body/eval_jaxpr/ppermute | solution.py:12
  356.6 5.8 %collective-permute-start = (bf16[1,2,24,576]{3,2,1,0:T(8,128)(2,1)S(1)}, bf16[1,2,24,576]{3,2,1,0:T(8,128)(2,1)S(1)}, u32[]{:S(2)}, u32[]{:S(2)}) collective-permute-start(bf16[1,2,24,576]{3,2,1,0:T(8,128)(2,1)S(1)} %get-tuple-element.598), channel_id=1, source_target_pairs={{0,1},{1,2},{2,3},{3,4},{4,5},{5,6},{6,7},{7,8},{8,9},{9,10},{10,1... | collective-permute-start | bytes 165896 | tf_op jit(solution)/shard_map/while/body/eval_jaxpr/ppermute | solution.py:12
  372.6 5.8 %collective-permute-start = (bf16[1,2,24,576]{3,2,1,0:T(8,128)(2,1)S(1)}, bf16[1,2,24,576]{3,2,1,0:T(8,128)(2,1)S(1)}, u32[]{:S(2)}, u32[]{:S(2)}) collective-permute-start(bf16[1,2,24,576]{3,2,1,0:T(8,128)(2,1)S(1)} %get-tuple-element.598), channel_id=1, source_target_pairs={{0,1},{1,2},{2,3},{3,4},{4,5},{5,6},{6,7},{7,8},{8,9},{9,10},{10,1... | collective-permute-start | bytes 165896 | tf_op jit(solution)/shard_map/while/body/eval_jaxpr/ppermute | solution.py:12
  388.5 5.8 %collective-permute-start = (bf16[1,2,24,576]{3,2,1,0:T(8,128)(2,1)S(1)}, bf16[1,2,24,576]{3,2,1,0:T(8,128)(2,1)S(1)}, u32[]{:S(2)}, u32[]{:S(2)}) collective-permute-start(bf16[1,2,24,576]{3,2,1,0:T(8,128)(2,1)S(1)} %get-tuple-element.598), channel_id=1, source_target_pairs={{0,1},{1,2},{2,3},{3,4},{4,5},{5,6},{6,7},{7,8},{8,9},{9,10},{10,1... | collective-permute-start | bytes 165896 | tf_op jit(solution)/shard_map/while/body/eval_jaxpr/ppermute | solution.py:12
  404.5 5.8 %collective-permute-start = (bf16[1,2,24,576]{3,2,1,0:T(8,128)(2,1)S(1)}, bf16[1,2,24,576]{3,2,1,0:T(8,128)(2,1)S(1)}, u32[]{:S(2)}, u32[]{:S(2)}) collective-permute-start(bf16[1,2,24,576]{3,2,1,0:T(8,128)(2,1)S(1)} %get-tuple-element.598), channel_id=1, source_target_pairs={{0,1},{1,2},{2,3},{3,4},{4,5},{5,6},{6,7},{7,8},{8,9},{9,10},{10,1... | collective-permute-start | bytes 165896 | tf_op jit(solution)/shard_map/while/body/eval_jaxpr/ppermute | solution.py:12
  420.5 5.8 %collective-permute-start = (bf16[1,2,24,576]{3,2,1,0:T(8,128)(2,1)S(1)}, bf16[1,2,24,576]{3,2,1,0:T(8,128)(2,1)S(1)}, u32[]{:S(2)}, u32[]{:S(2)}) collective-permute-start(bf16[1,2,24,576]{3,2,1,0:T(8,128)(2,1)S(1)} %get-tuple-element.598), channel_id=1, source_target_pairs={{0,1},{1,2},{2,3},{3,4},{4,5},{5,6},{6,7},{7,8},{8,9},{9,10},{10,1... | collective-permute-start | bytes 165896 | tf_op jit(solution)/shard_map/while/body/eval_jaxpr/ppermute | solution.py:12
  436.5 5.8 %collective-permute-start = (bf16[1,2,24,576]{3,2,1,0:T(8,128)(2,1)S(1)}, bf16[1,2,24,576]{3,2,1,0:T(8,128)(2,1)S(1)}, u32[]{:S(2)}, u32[]{:S(2)}) collective-permute-start(bf16[1,2,24,576]{3,2,1,0:T(8,128)(2,1)S(1)} %get-tuple-element.598), channel_id=1, source_target_pairs={{0,1},{1,2},{2,3},{3,4},{4,5},{5,6},{6,7},{7,8},{8,9},{9,10},{10,1... | collective-permute-start | bytes 165896 | tf_op jit(solution)/shard_map/while/body/eval_jaxpr/ppermute | solution.py:12
  452.4 5.8 %collective-permute-start = (bf16[1,2,24,576]{3,2,1,0:T(8,128)(2,1)S(1)}, bf16[1,2,24,576]{3,2,1,0:T(8,128)(2,1)S(1)}, u32[]{:S(2)}, u32[]{:S(2)}) collective-permute-start(bf16[1,2,24,576]{3,2,1,0:T(8,128)(2,1)S(1)} %get-tuple-element.598), channel_id=1, source_target_pairs={{0,1},{1,2},{2,3},{3,4},{4,5},{5,6},{6,7},{7,8},{8,9},{9,10},{10,1... | collective-permute-start | bytes 165896 | tf_op jit(solution)/shard_map/while/body/eval_jaxpr/ppermute | solution.py:12
  468.4 5.8 %collective-permute-start = (bf16[1,2,24,576]{3,2,1,0:T(8,128)(2,1)S(1)}, bf16[1,2,24,576]{3,2,1,0:T(8,128)(2,1)S(1)}, u32[]{:S(2)}, u32[]{:S(2)}) collective-permute-start(bf16[1,2,24,576]{3,2,1,0:T(8,128)(2,1)S(1)} %get-tuple-element.598), channel_id=1, source_target_pairs={{0,1},{1,2},{2,3},{3,4},{4,5},{5,6},{6,7},{7,8},{8,9},{9,10},{10,1... | collective-permute-start | bytes 165896 | tf_op jit(solution)/shard_map/while/body/eval_jaxpr/ppermute | solution.py:12
  484.4 5.8 %collective-permute-start = (bf16[1,2,24,576]{3,2,1,0:T(8,128)(2,1)S(1)}, bf16[1,2,24,576]{3,2,1,0:T(8,128)(2,1)S(1)}, u32[]{:S(2)}, u32[]{:S(2)}) collective-permute-start(bf16[1,2,24,576]{3,2,1,0:T(8,128)(2,1)S(1)} %get-tuple-element.598), channel_id=1, source_target_pairs={{0,1},{1,2},{2,3},{3,4},{4,5},{5,6},{6,7},{7,8},{8,9},{9,10},{10,1... | collective-permute-start | bytes 165896 | tf_op jit(solution)/shard_map/while/body/eval_jaxpr/ppermute | solution.py:12
  500.4 5.8 %collective-permute-start = (bf16[1,2,24,576]{3,2,1,0:T(8,128)(2,1)S(1)}, bf16[1,2,24,576]{3,2,1,0:T(8,128)(2,1)S(1)}, u32[]{:S(2)}, u32[]{:S(2)}) collective-permute-start(bf16[1,2,24,576]{3,2,1,0:T(8,128)(2,1)S(1)} %get-tuple-element.598), channel_id=1, source_target_pairs={{0,1},{1,2},{2,3},{3,4},{4,5},{5,6},{6,7},{7,8},{8,9},{9,10},{10,1... | collective-permute-start | bytes 165896 | tf_op jit(solution)/shard_map/while/body/eval_jaxpr/ppermute | solution.py:12
  516.3 5.8 %collective-permute-start = (bf16[1,2,24,576]{3,2,1,0:T(8,128)(2,1)S(1)}, bf16[1,2,24,576]{3,2,1,0:T(8,128)(2,1)S(1)}, u32[]{:S(2)}, u32[]{:S(2)}) collective-permute-start(bf16[1,2,24,576]{3,2,1,0:T(8,128)(2,1)S(1)} %get-tuple-element.598), channel_id=1, source_target_pairs={{0,1},{1,2},{2,3},{3,4},{4,5},{5,6},{6,7},{7,8},{8,9},{9,10},{10,1... | collective-permute-start | bytes 165896 | tf_op jit(solution)/shard_map/while/body/eval_jaxpr/ppermute | solution.py:12
  532.3 5.8 %collective-permute-start = (bf16[1,2,24,576]{3,2,1,0:T(8,128)(2,1)S(1)}, bf16[1,2,24,576]{3,2,1,0:T(8,128)(2,1)S(1)}, u32[]{:S(2)}, u32[]{:S(2)}) collective-permute-start(bf16[1,2,24,576]{3,2,1,0:T(8,128)(2,1)S(1)} %get-tuple-element.598), channel_id=1, source_target_pairs={{0,1},{1,2},{2,3},{3,4},{4,5},{5,6},{6,7},{7,8},{8,9},{9,10},{10,1... | collective-permute-start | bytes 165896 | tf_op jit(solution)/shard_map/while/body/eval_jaxpr/ppermute | solution.py:12
  (2 other events, 2.3 us)
where the time goes:
time: 551 us; the launch traced here: 549 us
  matrix products  200 us (36%)
  local copies, waits for them, and re-layouts  154 us (28%)
  waiting for transfers between devices  77 us (14%)
  loops' own time  72.5 us (13%)
  blocking collectives  35.1 us (6%)
    dot_general x768, matrix products, rotate_apply(): lax.dot_general(source_field, matrix, (((1,), (1,)), ((), ())), precision...  200 us
    ppermute x31, waiting for transfers between devices, passed_along(): lax.ppermute(array, axis, [(i, (i + by) % peers) for i in range(peers)])  77 us
    another operation x1, loops' own time, shards(): current, totals = lax.fori_loop(1, band_count, onward, (visitor, totals))  72.5 us
    sub x384, local copies, waits for them, and re-layouts, transform(): rotate_apply(real_part, cosine_table)  55.1 us
    add x384, local copies, waits for them, and re-layouts, transform(): rotate_apply(imag_part, cosine_table)  55.1 us
    dynamic_slice x32, local copies, waits for them, and re-layouts, contribute(): table_row = kernel_index[kpoint, source_k]  41.6 us
    all_gather x1, blocking collectives, shards(): everyone = lax.all_gather(occupied, 'ka', axis=0, tiled=True)  35.1 us
  transfers between devices with their start and end apart: 31, of which 31 were waited for; matrix products, arithmetic and copies ran while one was open for 7% of the time, Pallas kernels for 0%

commit v1 on v0

--- a/solution.py
+++ b/solution.py
@@ -66,7 +66,9 @@
     cosine_table, sine_table = spectral_tables(GRID)
     target_real = targets[:, 0]
     target_imag = targets[:, 1]
-    everyone = lax.all_gather(occupied, "ka", axis=0, tiled=True)
+    everyone = jnp.concatenate(
+        lax.all_to_all(jnp.stack([occupied] * lax.axis_size("ka")), "ka", 0, 0), axis=0
+    )
     partner_group = partner[my_group]
     visitor = lax.dynamic_slice_in_dim(everyone, partner_group, 1, 0)
 

time: 551 us -> 529 us (0.960)
  blocking collectives: 35.1 us -> 0 us
  starting transfers between devices: 2.58 us -> 10 us
    all_gather x1 -> x0, blocking collectives: 35.1 us -> none  [shards(): everyone = lax.all_gather(occupied, 'ka', axis=0, tiled=True)]
    all_to_all x0 -> x1, starting transfers between devices: none -> 7.46 us  [shards(): lax.all_to_all(jnp.stack([occupied] * lax.axis_size('ka')), 'ka', 0, 0)]
  transfers between devices with their start and end apart: 31 -> 32, of which waited for: 31 -> 32; matrix products, arithmetic and copies ran while one was open for 7% -> 8% of each run, Pallas kernels for 0% -> 0%
where the time goes in v1:
time: 529 us; the launch traced here: 526 us
  matrix products  200 us (38%)
  local copies, waits for them, and re-layouts  156 us (29%)
  waiting for transfers between devices  80.3 us (15%)
  loops' own time  71.2 us (13%)
  starting transfers between devices  10 us (2%)
    dot_general x768, matrix products, rotate_apply(): lax.dot_general(source_field, matrix, (((1,), (1,)), ((), ())), precision...  200 us
    ppermute x31, waiting for transfers between devices, passed_along(): lax.ppermute(array, axis, [(i, (i + by) % peers) for i in range(peers)])  77.3 us
    another operation x1, loops' own time, shards(): current, totals = lax.fori_loop(1, band_count, onward, (visitor, totals))  71.2 us
    add x384, local copies, waits for them, and re-layouts, transform(): rotate_apply(imag_part, cosine_table)  55.1 us
    sub x384, local copies, waits for them, and re-layouts, transform(): rotate_apply(real_part, cosine_table)  55.1 us
    dynamic_slice x32, local copies, waits for them, and re-layouts, contribute(): table_row = kernel_index[kpoint, source_k]  42.9 us
  transfers between devices with their start and end apart: 32, of which 32 were waited for; matrix products, arithmetic and copies ran while one was open for 8% of the time, Pallas kernels for 0%

profile of v1, /device:TPU:2, one launch (start us, length us, event | category | flops | bytes accessed | tf_op | source)
XLA Modules:
  0.0 525.6 jit_solution(11325345018465727485)
XLA Ops:
  1.7 7.5 %all-to-all-start = ((bf16[8,1,2,24,576]{4,3,2,1,0:T(8,128)(2,1)}), bf16[8,1,2,24,576]{4,3,2,1,0:T(8,128)(2,1)S(1)}, u32[]{:S(2)}, u32[]{:S(2)}) async-start(bf16[8,1,2,24,576]{4,3,2,1,0:T(8,128)(2,1)} %stack.8), calls=%async_computation | async-start | bytes 983040 | tf_op jit(solution)/shard_map/all_to_all | solution.py:70
  16.2 2.9 all-to-all-done
  29.3 495.6 %while.21 = (s32[]{:T(128)}, bf16[1,2,24,576]{3,2,1,0:T(8,128)(2,1)S(1)}, f32[1,24,576]{2,1,0:T(8,128)S(1)}, f32[1,24,576]{2,1,0:T(8,128)S(1)}, s32[]{:T(128)}, ...) while((s32[]{:T(128)}, ...), condition=%wide.region_1.2_spmd.clone.clone, body=%wide.region_0.1_spmd.clone.clone.sunk | while | flops 96215040 | bytes 7526992 | solution.py:92
  32.9 2.8 collective-permute-done
  49.2 2.5 collective-permute-done
  65.1 2.5 collective-permute-done
  81.1 2.5 collective-permute-done
  97.1 2.5 collective-permute-done
  113.0 2.5 collective-permute-done
  129.0 2.5 collective-permute-done
  145.0 2.5 collective-permute-done
  161.0 2.5 collective-permute-done
  176.9 2.5 collective-permute-done
  192.9 2.5 collective-permute-done
  208.9 2.5 collective-permute-done
  224.8 2.5 collective-permute-done
  240.8 2.5 collective-permute-done
  256.8 2.5 collective-permute-done
  272.7 2.5 collective-permute-done
  288.7 2.5 collective-permute-done
  304.7 2.5 collective-permute-done
  320.7 2.5 collective-permute-done
  336.6 2.5 collective-permute-done
  352.6 2.5 collective-permute-done
  368.6 2.5 collective-permute-done
  384.5 2.5 collective-permute-done
  400.5 2.5 collective-permute-done
  416.5 2.5 collective-permute-done
  432.5 2.5 collective-permute-done
  448.4 2.5 collective-permute-done
  464.4 2.5 collective-permute-done
  480.4 2.5 collective-permute-done
  (1737 shorter events, 366.7 us)
Async XLA Ops:
  1.7 17.5 %all-to-all-start = ((bf16[8,1,2,24,576]{4,3,2,1,0:T(8,128)(2,1)}), bf16[8,1,2,24,576]{4,3,2,1,0:T(8,128)(2,1)S(1)}, u32[]{:S(2)}, u32[]{:S(2)}) async-start(bf16[8,1,2,24,576]{4,3,2,1,0:T(8,128)(2,1)} %stack.8), calls=%async_computation | async-start | bytes 983040 | tf_op jit(solution)/shard_map/all_to_all | solution.py:70
  29.5 6.2 %collective-permute-start = (bf16[1,2,24,576]{3,2,1,0:T(8,128)(2,1)S(1)}, bf16[1,2,24,576]{3,2,1,0:T(8,128)(2,1)S(1)}, u32[]{:S(2)}, u32[]{:S(2)}) collective-permute-start(bf16[1,2,24,576]{3,2,1,0:T(8,128)(2,1)S(1)} %get-tuple-element.598), channel_id=1, source_target_pairs={{0,1},{1,2},{2,3},{3,4},{4,5},{5,6},{6,7},{7,8},{8,9},{9,10},{10,1... | collective-permute-start | bytes 165896 | tf_op jit(solution)/shard_map/while/body/eval_jaxpr/ppermute | solution.py:12
  45.8 5.8 %collective-permute-start = (bf16[1,2,24,576]{3,2,1,0:T(8,128)(2,1)S(1)}, bf16[1,2,24,576]{3,2,1,0:T(8,128)(2,1)S(1)}, u32[]{:S(2)}, u32[]{:S(2)}) collective-permute-start(bf16[1,2,24,576]{3,2,1,0:T(8,128)(2,1)S(1)} %get-tuple-element.598), channel_id=1, source_target_pairs={{0,1},{1,2},{2,3},{3,4},{4,5},{5,6},{6,7},{7,8},{8,9},{9,10},{10,1... | collective-permute-start | bytes 165896 | tf_op jit(solution)/shard_map/while/body/eval_jaxpr/ppermute | solution.py:12
  61.8 5.8 %collective-permute-start = (bf16[1,2,24,576]{3,2,1,0:T(8,128)(2,1)S(1)}, bf16[1,2,24,576]{3,2,1,0:T(8,128)(2,1)S(1)}, u32[]{:S(2)}, u32[]{:S(2)}) collective-permute-start(bf16[1,2,24,576]{3,2,1,0:T(8,128)(2,1)S(1)} %get-tuple-element.598), channel_id=1, source_target_pairs={{0,1},{1,2},{2,3},{3,4},{4,5},{5,6},{6,7},{7,8},{8,9},{9,10},{10,1... | collective-permute-start | bytes 165896 | tf_op jit(solution)/shard_map/while/body/eval_jaxpr/ppermute | solution.py:12
  77.7 5.8 %collective-permute-start = (bf16[1,2,24,576]{3,2,1,0:T(8,128)(2,1)S(1)}, bf16[1,2,24,576]{3,2,1,0:T(8,128)(2,1)S(1)}, u32[]{:S(2)}, u32[]{:S(2)}) collective-permute-start(bf16[1,2,24,576]{3,2,1,0:T(8,128)(2,1)S(1)} %get-tuple-element.598), channel_id=1, source_target_pairs={{0,1},{1,2},{2,3},{3,4},{4,5},{5,6},{6,7},{7,8},{8,9},{9,10},{10,1... | collective-permute-start | bytes 165896 | tf_op jit(solution)/shard_map/while/body/eval_jaxpr/ppermute | solution.py:12
  93.7 5.8 %collective-permute-start = (bf16[1,2,24,576]{3,2,1,0:T(8,128)(2,1)S(1)}, bf16[1,2,24,576]{3,2,1,0:T(8,128)(2,1)S(1)}, u32[]{:S(2)}, u32[]{:S(2)}) collective-permute-start(bf16[1,2,24,576]{3,2,1,0:T(8,128)(2,1)S(1)} %get-tuple-element.598), channel_id=1, source_target_pairs={{0,1},{1,2},{2,3},{3,4},{4,5},{5,6},{6,7},{7,8},{8,9},{9,10},{10,1... | collective-permute-start | bytes 165896 | tf_op jit(solution)/shard_map/while/body/eval_jaxpr/ppermute | solution.py:12
  109.7 5.8 %collective-permute-start = (bf16[1,2,24,576]{3,2,1,0:T(8,128)(2,1)S(1)}, bf16[1,2,24,576]{3,2,1,0:T(8,128)(2,1)S(1)}, u32[]{:S(2)}, u32[]{:S(2)}) collective-permute-start(bf16[1,2,24,576]{3,2,1,0:T(8,128)(2,1)S(1)} %get-tuple-element.598), channel_id=1, source_target_pairs={{0,1},{1,2},{2,3},{3,4},{4,5},{5,6},{6,7},{7,8},{8,9},{9,10},{10,1... | collective-permute-start | bytes 165896 | tf_op jit(solution)/shard_map/while/body/eval_jaxpr/ppermute | solution.py:12
  125.7 5.8 %collective-permute-start = (bf16[1,2,24,576]{3,2,1,0:T(8,128)(2,1)S(1)}, bf16[1,2,24,576]{3,2,1,0:T(8,128)(2,1)S(1)}, u32[]{:S(2)}, u32[]{:S(2)}) collective-permute-start(bf16[1,2,24,576]{3,2,1,0:T(8,128)(2,1)S(1)} %get-tuple-element.598), channel_id=1, source_target_pairs={{0,1},{1,2},{2,3},{3,4},{4,5},{5,6},{6,7},{7,8},{8,9},{9,10},{10,1... | collective-permute-start | bytes 165896 | tf_op jit(solution)/shard_map/while/body/eval_jaxpr/ppermute | solution.py:12
  141.6 5.8 %collective-permute-start = (bf16[1,2,24,576]{3,2,1,0:T(8,128)(2,1)S(1)}, bf16[1,2,24,576]{3,2,1,0:T(8,128)(2,1)S(1)}, u32[]{:S(2)}, u32[]{:S(2)}) collective-permute-start(bf16[1,2,24,576]{3,2,1,0:T(8,128)(2,1)S(1)} %get-tuple-element.598), channel_id=1, source_target_pairs={{0,1},{1,2},{2,3},{3,4},{4,5},{5,6},{6,7},{7,8},{8,9},{9,10},{10,1... | collective-permute-start | bytes 165896 | tf_op jit(solution)/shard_map/while/body/eval_jaxpr/ppermute | solution.py:12
  157.6 5.8 %collective-permute-start = (bf16[1,2,24,576]{3,2,1,0:T(8,128)(2,1)S(1)}, bf16[1,2,24,576]{3,2,1,0:T(8,128)(2,1)S(1)}, u32[]{:S(2)}, u32[]{:S(2)}) collective-permute-start(bf16[1,2,24,576]{3,2,1,0:T(8,128)(2,1)S(1)} %get-tuple-element.598), channel_id=1, source_target_pairs={{0,1},{1,2},{2,3},{3,4},{4,5},{5,6},{6,7},{7,8},{8,9},{9,10},{10,1... | collective-permute-start | bytes 165896 | tf_op jit(solution)/shard_map/while/body/eval_jaxpr/ppermute | solution.py:12
  173.6 5.8 %collective-permute-start = (bf16[1,2,24,576]{3,2,1,0:T(8,128)(2,1)S(1)}, bf16[1,2,24,576]{3,2,1,0:T(8,128)(2,1)S(1)}, u32[]{:S(2)}, u32[]{:S(2)}) collective-permute-start(bf16[1,2,24,576]{3,2,1,0:T(8,128)(2,1)S(1)} %get-tuple-element.598), channel_id=1, source_target_pairs={{0,1},{1,2},{2,3},{3,4},{4,5},{5,6},{6,7},{7,8},{8,9},{9,10},{10,1... | collective-permute-start | bytes 165896 | tf_op jit(solution)/shard_map/while/body/eval_jaxpr/ppermute | solution.py:12
  189.5 5.8 %collective-permute-start = (bf16[1,2,24,576]{3,2,1,0:T(8,128)(2,1)S(1)}, bf16[1,2,24,576]{3,2,1,0:T(8,128)(2,1)S(1)}, u32[]{:S(2)}, u32[]{:S(2)}) collective-permute-start(bf16[1,2,24,576]{3,2,1,0:T(8,128)(2,1)S(1)} %get-tuple-element.598), channel_id=1, source_target_pairs={{0,1},{1,2},{2,3},{3,4},{4,5},{5,6},{6,7},{7,8},{8,9},{9,10},{10,1... | collective-permute-start | bytes 165896 | tf_op jit(solution)/shard_map/while/body/eval_jaxpr/ppermute | solution.py:12
  205.5 5.8 %collective-permute-start = (bf16[1,2,24,576]{3,2,1,0:T(8,128)(2,1)S(1)}, bf16[1,2,24,576]{3,2,1,0:T(8,128)(2,1)S(1)}, u32[]{:S(2)}, u32[]{:S(2)}) collective-permute-start(bf16[1,2,24,576]{3,2,1,0:T(8,128)(2,1)S(1)} %get-tuple-element.598), channel_id=1, source_target_pairs={{0,1},{1,2},{2,3},{3,4},{4,5},{5,6},{6,7},{7,8},{8,9},{9,10},{10,1... | collective-permute-start | bytes 165896 | tf_op jit(solution)/shard_map/while/body/eval_jaxpr/ppermute | solution.py:12
  221.5 5.8 %collective-permute-start = (bf16[1,2,24,576]{3,2,1,0:T(8,128)(2,1)S(1)}, bf16[1,2,24,576]{3,2,1,0:T(8,128)(2,1)S(1)}, u32[]{:S(2)}, u32[]{:S(2)}) collective-permute-start(bf16[1,2,24,576]{3,2,1,0:T(8,128)(2,1)S(1)} %get-tuple-element.598), channel_id=1, source_target_pairs={{0,1},{1,2},{2,3},{3,4},{4,5},{5,6},{6,7},{7,8},{8,9},{9,10},{10,1... | collective-permute-start | bytes 165896 | tf_op jit(solution)/shard_map/while/body/eval_jaxpr/ppermute | solution.py:12
  237.5 5.8 %collective-permute-start = (bf16[1,2,24,576]{3,2,1,0:T(8,128)(2,1)S(1)}, bf16[1,2,24,576]{3,2,1,0:T(8,128)(2,1)S(1)}, u32[]{:S(2)}, u32[]{:S(2)}) collective-permute-start(bf16[1,2,24,576]{3,2,1,0:T(8,128)(2,1)S(1)} %get-tuple-element.598), channel_id=1, source_target_pairs={{0,1},{1,2},{2,3},{3,4},{4,5},{5,6},{6,7},{7,8},{8,9},{9,10},{10,1... | collective-permute-start | bytes 165896 | tf_op jit(solution)/shard_map/while/body/eval_jaxpr/ppermute | solution.py:12
  253.4 5.8 %collective-permute-start = (bf16[1,2,24,576]{3,2,1,0:T(8,128)(2,1)S(1)}, bf16[1,2,24,576]{3,2,1,0:T(8,128)(2,1)S(1)}, u32[]{:S(2)}, u32[]{:S(2)}) collective-permute-start(bf16[1,2,24,576]{3,2,1,0:T(8,128)(2,1)S(1)} %get-tuple-element.598), channel_id=1, source_target_pairs={{0,1},{1,2},{2,3},{3,4},{4,5},{5,6},{6,7},{7,8},{8,9},{9,10},{10,1... | collective-permute-start | bytes 165896 | tf_op jit(solution)/shard_map/while/body/eval_jaxpr/ppermute | solution.py:12
  269.4 5.8 %collective-permute-start = (bf16[1,2,24,576]{3,2,1,0:T(8,128)(2,1)S(1)}, bf16[1,2,24,576]{3,2,1,0:T(8,128)(2,1)S(1)}, u32[]{:S(2)}, u32[]{:S(2)}) collective-permute-start(bf16[1,2,24,576]{3,2,1,0:T(8,128)(2,1)S(1)} %get-tuple-element.598), channel_id=1, source_target_pairs={{0,1},{1,2},{2,3},{3,4},{4,5},{5,6},{6,7},{7,8},{8,9},{9,10},{10,1... | collective-permute-start | bytes 165896 | tf_op jit(solution)/shard_map/while/body/eval_jaxpr/ppermute | solution.py:12
  285.4 5.8 %collective-permute-start = (bf16[1,2,24,576]{3,2,1,0:T(8,128)(2,1)S(1)}, bf16[1,2,24,576]{3,2,1,0:T(8,128)(2,1)S(1)}, u32[]{:S(2)}, u32[]{:S(2)}) collective-permute-start(bf16[1,2,24,576]{3,2,1,0:T(8,128)(2,1)S(1)} %get-tuple-element.598), channel_id=1, source_target_pairs={{0,1},{1,2},{2,3},{3,4},{4,5},{5,6},{6,7},{7,8},{8,9},{9,10},{10,1... | collective-permute-start | bytes 165896 | tf_op jit(solution)/shard_map/while/body/eval_jaxpr/ppermute | solution.py:12
  301.3 5.8 %collective-permute-start = (bf16[1,2,24,576]{3,2,1,0:T(8,128)(2,1)S(1)}, bf16[1,2,24,576]{3,2,1,0:T(8,128)(2,1)S(1)}, u32[]{:S(2)}, u32[]{:S(2)}) collective-permute-start(bf16[1,2,24,576]{3,2,1,0:T(8,128)(2,1)S(1)} %get-tuple-element.598), channel_id=1, source_target_pairs={{0,1},{1,2},{2,3},{3,4},{4,5},{5,6},{6,7},{7,8},{8,9},{9,10},{10,1... | collective-permute-start | bytes 165896 | tf_op jit(solution)/shard_map/while/body/eval_jaxpr/ppermute | solution.py:12
  317.3 5.8 %collective-permute-start = (bf16[1,2,24,576]{3,2,1,0:T(8,128)(2,1)S(1)}, bf16[1,2,24,576]{3,2,1,0:T(8,128)(2,1)S(1)}, u32[]{:S(2)}, u32[]{:S(2)}) collective-permute-start(bf16[1,2,24,576]{3,2,1,0:T(8,128)(2,1)S(1)} %get-tuple-element.598), channel_id=1, source_target_pairs={{0,1},{1,2},{2,3},{3,4},{4,5},{5,6},{6,7},{7,8},{8,9},{9,10},{10,1... | collective-permute-start | bytes 165896 | tf_op jit(solution)/shard_map/while/body/eval_jaxpr/ppermute | solution.py:12
  333.3 5.8 %collective-permute-start = (bf16[1,2,24,576]{3,2,1,0:T(8,128)(2,1)S(1)}, bf16[1,2,24,576]{3,2,1,0:T(8,128)(2,1)S(1)}, u32[]{:S(2)}, u32[]{:S(2)}) collective-permute-start(bf16[1,2,24,576]{3,2,1,0:T(8,128)(2,1)S(1)} %get-tuple-element.598), channel_id=1, source_target_pairs={{0,1},{1,2},{2,3},{3,4},{4,5},{5,6},{6,7},{7,8},{8,9},{9,10},{10,1... | collective-permute-start | bytes 165896 | tf_op jit(solution)/shard_map/while/body/eval_jaxpr/ppermute | solution.py:12
  349.3 5.8 %collective-permute-start = (bf16[1,2,24,576]{3,2,1,0:T(8,128)(2,1)S(1)}, bf16[1,2,24,576]{3,2,1,0:T(8,128)(2,1)S(1)}, u32[]{:S(2)}, u32[]{:S(2)}) collective-permute-start(bf16[1,2,24,576]{3,2,1,0:T(8,128)(2,1)S(1)} %get-tuple-element.598), channel_id=1, source_target_pairs={{0,1},{1,2},{2,3},{3,4},{4,5},{5,6},{6,7},{7,8},{8,9},{9,10},{10,1... | collective-permute-start | bytes 165896 | tf_op jit(solution)/shard_map/while/body/eval_jaxpr/ppermute | solution.py:12
  365.2 5.8 %collective-permute-start = (bf16[1,2,24,576]{3,2,1,0:T(8,128)(2,1)S(1)}, bf16[1,2,24,576]{3,2,1,0:T(8,128)(2,1)S(1)}, u32[]{:S(2)}, u32[]{:S(2)}) collective-permute-start(bf16[1,2,24,576]{3,2,1,0:T(8,128)(2,1)S(1)} %get-tuple-element.598), channel_id=1, source_target_pairs={{0,1},{1,2},{2,3},{3,4},{4,5},{5,6},{6,7},{7,8},{8,9},{9,10},{10,1... | collective-permute-start | bytes 165896 | tf_op jit(solution)/shard_map/while/body/eval_jaxpr/ppermute | solution.py:12
  381.2 5.8 %collective-permute-start = (bf16[1,2,24,576]{3,2,1,0:T(8,128)(2,1)S(1)}, bf16[1,2,24,576]{3,2,1,0:T(8,128)(2,1)S(1)}, u32[]{:S(2)}, u32[]{:S(2)}) collective-permute-start(bf16[1,2,24,576]{3,2,1,0:T(8,128)(2,1)S(1)} %get-tuple-element.598), channel_id=1, source_target_pairs={{0,1},{1,2},{2,3},{3,4},{4,5},{5,6},{6,7},{7,8},{8,9},{9,10},{10,1... | collective-permute-start | bytes 165896 | tf_op jit(solution)/shard_map/while/body/eval_jaxpr/ppermute | solution.py:12
  397.2 5.8 %collective-permute-start = (bf16[1,2,24,576]{3,2,1,0:T(8,128)(2,1)S(1)}, bf16[1,2,24,576]{3,2,1,0:T(8,128)(2,1)S(1)}, u32[]{:S(2)}, u32[]{:S(2)}) collective-permute-start(bf16[1,2,24,576]{3,2,1,0:T(8,128)(2,1)S(1)} %get-tuple-element.598), channel_id=1, source_target_pairs={{0,1},{1,2},{2,3},{3,4},{4,5},{5,6},{6,7},{7,8},{8,9},{9,10},{10,1... | collective-permute-start | bytes 165896 | tf_op jit(solution)/shard_map/while/body/eval_jaxpr/ppermute | solution.py:12
  413.1 5.8 %collective-permute-start = (bf16[1,2,24,576]{3,2,1,0:T(8,128)(2,1)S(1)}, bf16[1,2,24,576]{3,2,1,0:T(8,128)(2,1)S(1)}, u32[]{:S(2)}, u32[]{:S(2)}) collective-permute-start(bf16[1,2,24,576]{3,2,1,0:T(8,128)(2,1)S(1)} %get-tuple-element.598), channel_id=1, source_target_pairs={{0,1},{1,2},{2,3},{3,4},{4,5},{5,6},{6,7},{7,8},{8,9},{9,10},{10,1... | collective-permute-start | bytes 165896 | tf_op jit(solution)/shard_map/while/body/eval_jaxpr/ppermute | solution.py:12
  429.1 5.8 %collective-permute-start = (bf16[1,2,24,576]{3,2,1,0:T(8,128)(2,1)S(1)}, bf16[1,2,24,576]{3,2,1,0:T(8,128)(2,1)S(1)}, u32[]{:S(2)}, u32[]{:S(2)}) collective-permute-start(bf16[1,2,24,576]{3,2,1,0:T(8,128)(2,1)S(1)} %get-tuple-element.598), channel_id=1, source_target_pairs={{0,1},{1,2},{2,3},{3,4},{4,5},{5,6},{6,7},{7,8},{8,9},{9,10},{10,1... | collective-permute-start | bytes 165896 | tf_op jit(solution)/shard_map/while/body/eval_jaxpr/ppermute | solution.py:12
  445.1 5.8 %collective-permute-start = (bf16[1,2,24,576]{3,2,1,0:T(8,128)(2,1)S(1)}, bf16[1,2,24,576]{3,2,1,0:T(8,128)(2,1)S(1)}, u32[]{:S(2)}, u32[]{:S(2)}) collective-permute-start(bf16[1,2,24,576]{3,2,1,0:T(8,128)(2,1)S(1)} %get-tuple-element.598), channel_id=1, source_target_pairs={{0,1},{1,2},{2,3},{3,4},{4,5},{5,6},{6,7},{7,8},{8,9},{9,10},{10,1... | collective-permute-start | bytes 165896 | tf_op jit(solution)/shard_map/while/body/eval_jaxpr/ppermute | solution.py:12
  461.0 5.8 %collective-permute-start = (bf16[1,2,24,576]{3,2,1,0:T(8,128)(2,1)S(1)}, bf16[1,2,24,576]{3,2,1,0:T(8,128)(2,1)S(1)}, u32[]{:S(2)}, u32[]{:S(2)}) collective-permute-start(bf16[1,2,24,576]{3,2,1,0:T(8,128)(2,1)S(1)} %get-tuple-element.598), channel_id=1, source_target_pairs={{0,1},{1,2},{2,3},{3,4},{4,5},{5,6},{6,7},{7,8},{8,9},{9,10},{10,1... | collective-permute-start | bytes 165896 | tf_op jit(solution)/shard_map/while/body/eval_jaxpr/ppermute | solution.py:12
  477.0 5.8 %collective-permute-start = (bf16[1,2,24,576]{3,2,1,0:T(8,128)(2,1)S(1)}, bf16[1,2,24,576]{3,2,1,0:T(8,128)(2,1)S(1)}, u32[]{:S(2)}, u32[]{:S(2)}) collective-permute-start(bf16[1,2,24,576]{3,2,1,0:T(8,128)(2,1)S(1)} %get-tuple-element.598), channel_id=1, source_target_pairs={{0,1},{1,2},{2,3},{3,4},{4,5},{5,6},{6,7},{7,8},{8,9},{9,10},{10,1... | collective-permute-start | bytes 165896 | tf_op jit(solution)/shard_map/while/body/eval_jaxpr/ppermute | solution.py:12
  493.0 5.8 %collective-permute-start = (bf16[1,2,24,576]{3,2,1,0:T(8,128)(2,1)S(1)}, bf16[1,2,24,576]{3,2,1,0:T(8,128)(2,1)S(1)}, u32[]{:S(2)}, u32[]{:S(2)}) collective-permute-start(bf16[1,2,24,576]{3,2,1,0:T(8,128)(2,1)S(1)} %get-tuple-element.598), channel_id=1, source_target_pairs={{0,1},{1,2},{2,3},{3,4},{4,5},{5,6},{6,7},{7,8},{8,9},{9,10},{10,1... | collective-permute-start | bytes 165896 | tf_op jit(solution)/shard_map/while/body/eval_jaxpr/ppermute | solution.py:12
  509.0 5.8 %collective-permute-start = (bf16[1,2,24,576]{3,2,1,0:T(8,128)(2,1)S(1)}, bf16[1,2,24,576]{3,2,1,0:T(8,128)(2,1)S(1)}, u32[]{:S(2)}, u32[]{:S(2)}) collective-permute-start(bf16[1,2,24,576]{3,2,1,0:T(8,128)(2,1)S(1)} %get-tuple-element.598), channel_id=1, source_target_pairs={{0,1},{1,2},{2,3},{3,4},{4,5},{5,6},{6,7},{7,8},{8,9},{9,10},{10,1... | collective-permute-start | bytes 165896 | tf_op jit(solution)/shard_map/while/body/eval_jaxpr/ppermute | solution.py:12
  (3 other events, 5.0 us)
